TPU v7x, 512 devices: a whole 4x4x16 slice. The times are simulated.
512 devices in a mesh: row: 16 (over y, x_lo, core), col: 32 (over z, x_hi).
Axes of the slice: x: 4 (x_hi: 2, x_lo: 2; x = x_hi * 2 + x_lo), y: 4, z: 16, core: 2. Of those that a mesh axis runs over, the one named last changes fastest.
Arguments:
- traces: float32 [1024, 4096], P(('row', 'col')), may hold values from -6 to 6
- offsets: int32 [1024, 8], P(('row', 'col')), may hold values from 0 to 3072, as said below
- band_lo: int32 [1024], P(('row', 'col')), may hold values from 0 to 63
- band_hi: int32 [1024], P(('row', 'col')), may hold values from 192 to 256
- live: int32 [1024], P(('row', 'col')), may hold values 0 or 1
Outputs:
- correlations: bfloat16 [1024, 32, 16, 2, 512], P('row', 'col')
Inputs may be any that keep to these rules, and one draw needn't show every extreme that they name: `offsets`: every offset is a multiple of 256.
All inputs are finite; a program needn't handle non-finite values. No bound on the sum of `live` on one device may be relied on, other than what follows from the above.
Results may differ from a plain program's by a relative error of at most 0.0052.
Values may be sent and summed in bfloat16 or wider, within the bound.
A program may use at most 64 MiB of HBM per device.

v0:
```python
import math
import jax
import jax.numpy as jnp
from jax import lax
from jax.sharding import PartitionSpec as P

SEG = 8
SAMPLES = 1024
BINS = 256
LAGS = 512
TRACE = 4096


def sent_to_all(x, axis):
    devices = lax.axis_size(axis)
    return lax.all_to_all(jnp.broadcast_to(x[None], (devices, *x.shape)), axis, 0, 0, tiled=True)


def laid_out(pieces, dim):
    dims = list(pieces.shape[1:])
    dims[dim] *= pieces.shape[0]
    return jnp.moveaxis(pieces, 0, dim).reshape(dims)


def gather_directly(x, axis, dim):
    pieces = sent_to_all(x, axis)
    return laid_out(pieces, dim)


def transform_table():
    times = jnp.arange(SAMPLES, dtype=jnp.int32)
    freqs = jnp.arange(BINS, dtype=jnp.int32) + 1
    phase = jnp.mod(times[:, None] * freqs[None, :], SAMPLES).astype(jnp.float32) * (
        2.0 * math.pi / SAMPLES
    )
    taper = 0.5 - 0.5 * jnp.cos(times.astype(jnp.float32) * (2.0 * math.pi / SAMPLES))
    return jnp.concatenate([jnp.cos(phase), -jnp.sin(phase)], axis=1) * taper[:, None]


def lag_table():
    freqs = jnp.arange(BINS, dtype=jnp.int32) + 1
    shifts = jnp.arange(LAGS, dtype=jnp.int32) - LAGS // 2
    phase = jnp.mod(freqs[:, None] * shifts[None, :], SAMPLES).astype(jnp.float32) * (
        2.0 * math.pi / SAMPLES
    )
    return jnp.concatenate([jnp.cos(phase), -jnp.sin(phase)], axis=0) * (
        1.0 / math.sqrt(SEG * BINS)
    )


def cut_segments(traces, offsets):
    count = traces.shape[0]
    quarter = SAMPLES // 4
    block_count = TRACE // quarter
    blocks = traces.reshape(count, 1, block_count, quarter)
    first_block = offsets // quarter
    segment = jnp.zeros((count, SEG, 4, quarter), jnp.float32)
    for place in range(block_count - 3):
        picked = (first_block == place)[:, :, None, None]
        segment = jnp.where(picked, blocks[:, :, place : place + 4, :], segment)
    return segment.reshape(count * SEG, SAMPLES)


def whiten(traces, offsets, band_lo, band_hi, live):
    count = traces.shape[0]
    flat = cut_segments(traces, offsets)
    spec = jnp.dot(flat, transform_table(), precision=lax.Precision.HIGHEST)
    spec_re = spec[:, :BINS]
    spec_im = spec[:, BINS:]
    amp = jnp.sqrt(spec_re * spec_re + spec_im * spec_im)
    padded = jnp.pad(amp, ((0, 0), (2, 2)))
    smooth = (
        padded[:, 0:BINS]
        + padded[:, 1 : BINS + 1]
        + padded[:, 2 : BINS + 2]
        + padded[:, 3 : BINS + 3]
        + padded[:, 4 : BINS + 4]
    ) / 5.0
    level = jnp.mean(amp, axis=1, keepdims=True)
    factor = 1.0 / (smooth + 0.1 * level + 1e-06)
    bins = jnp.arange(BINS, dtype=jnp.int32)
    inside = (
        (bins[None, :] >= band_lo[:, None])
        & (bins[None, :] < band_hi[:, None])
        & (live[:, None] == 1)
    )
    keep = inside.astype(jnp.float32)
    factor = factor.reshape(count, SEG, BINS) * keep[:, None, :]
    spec = spec.reshape(count, SEG, 2 * BINS)
    white = spec * jnp.concatenate([factor, factor], axis=2)
    return white.astype(jnp.bfloat16)


def correlate(first, second, table):
    first_re, first_im = (first[..., :BINS], first[..., BINS:])
    second_re, second_im = (second[..., :BINS], second[..., BINS:])
    count_i, count_j = (first.shape[0], second.shape[0])
    cross_re = jnp.zeros((count_i, count_j, BINS), jnp.float32)
    cross_im = jnp.zeros((count_i, count_j, BINS), jnp.float32)
    for seg_index in range(SEG):
        left_re = first_re[:, None, seg_index, :].astype(jnp.float32)
        left_im = first_im[:, None, seg_index, :].astype(jnp.float32)
        right_re = second_re[None, :, seg_index, :].astype(jnp.float32)
        right_im = second_im[None, :, seg_index, :].astype(jnp.float32)
        cross_re = cross_re + (left_re * right_re + left_im * right_im)
        cross_im = cross_im + (left_im * right_re - left_re * right_im)
    cross = jnp.concatenate([cross_re, cross_im], axis=2)
    corr = jnp.dot(
        cross.reshape(count_i * count_j, 2 * BINS), table, precision=lax.Precision.HIGHEST
    )
    return corr.astype(jnp.bfloat16).reshape(count_i, count_j, LAGS)


def body(traces, offsets, band_lo, band_hi, live):
    white = whiten(traces, offsets, band_lo, band_hi, live)
    table = lag_table()
    first_panel = gather_directly(white, "col", 0)
    stacked = correlate(first_panel, lax.all_gather(white, "row", axis=0, tiled=True), table)
    channel_count = white.shape[0]
    return stacked.reshape(stacked.shape[0], 1, lax.axis_size("row"), channel_count, LAGS)


def solution(mesh):
    in_specs = (
        P(("row", "col"), None),
        P(("row", "col"), None),
        P(("row", "col")),
        P(("row", "col")),
        P(("row", "col")),
    )
    out_specs = P("row", "col", None, None, None)
    return jax.shard_map(body, mesh=mesh, in_specs=in_specs, out_specs=out_specs, check_vma=False)
```

profile of v0, /device:TPU:24, one launch (start us, length us, event | category | flops | bytes accessed | tf_op | source)
XLA Modules:
  0.0 75.8 jit_solution(12472655420938415955)
XLA Ops:
  0.0 0.7 broadcast_compare_fusion.13
  0.7 0.7 broadcast_compare_fusion.9
  1.4 0.1 broadcast_in_dim.248
  1.5 0.1 broadcast_in_dim.253
  1.6 0.1 broadcast_in_dim.303
  1.7 0.1 broadcast_in_dim.298
  1.8 0.1 broadcast_in_dim.293
  1.8 0.1 broadcast_in_dim.288
  1.9 0.1 broadcast_in_dim.283
  2.0 0.1 broadcast_in_dim.278
  2.1 0.1 broadcast_in_dim.273
  2.2 0.1 broadcast_in_dim.268
  2.3 0.1 broadcast_in_dim.263
  2.4 0.1 broadcast_in_dim.258
  2.4 0.1 broadcast_in_dim.308
  2.5 0.8 %copy.74 = f32[1,2,16,256]{3,2,1,0:T(8,128)S(1)} copy(f32[1,2,16,256]{3,1,2,0:T(2,128)} %bitcast.134) | data formatting | bytes 65536
  3.3 4.1 %fusion.23 = (f32[1024,256]{1,0:T(8,128)S(1)}, f32[1024,256]{1,0:T(8,128)S(1)}) fusion(s32[256]{0:T(256)S(1)} %iota_add_fusion.1), kind=kLoop, calls=%fused_computation.35 | loop fusion | flops 3932160 | bytes 2098176 | tf_op jit(solution)/shard_map/cos | solution.py:37
  7.4 0.0 copy-start
  7.4 0.0 copy-start.1
  7.6 1.3 %fusion.7 = f32[16,512]{1,0:T(8,128)S(1)} fusion(f32[1024,256]{1,0:T(8,128)S(1)} %get-tuple-element.69, f32[1024,256]{1,0:T(8,128)S(1)} %get-tuple-element.68, f32[1024]{0:T(1024)S(1)} %multiply_subtract_fusion, f32[16,1024]{1,0:T(8,128)S(1)} %bitcast.133, f32[16,1024]{1,0:T(8,128)S(1)} %bitcast.132, f32[16,1024]{1,0:T(8,128)S(1)} %bitcast.131, ...), kind=kOutput, calls=%fused_computation.6 | convolution fusion | flops 101924864 | bytes 2986192 | tf_op jit(solution)/shard_map/dot_general | solution.py:67
  9.0 0.1 fusion.67
  9.1 0.0 copy-done
  9.1 0.0 copy-done.1
  9.1 0.1 and_convert_fusion
  9.2 0.1 bitcast_multiply_fusion
  9.3 0.9 %broadcast_in_dim.314 = bf16[32,2,8,512]{3,2,1,0:T(8,128)(2,1)} broadcast(bf16[2,8,512]{2,1,0:T(8,128)(2,1)S(1)} %fusion.38), dimensions={1,2,3} | broadcast | bytes 540672 | tf_op jit(solution)/shard_map/broadcast_in_dim | solution.py:16
  10.2 17.9 %all-to-all-start = ((bf16[32,2,8,512]{3,2,1,0:T(8,128)(2,1)}), bf16[32,2,8,512]{3,2,1,0:T(8,128)(2,1)S(1)}, u32[]{:S(2)}, u32[]{:S(2)}) async-start(bf16[32,2,8,512]{3,2,1,0:T(8,128)(2,1)} %broadcast_in_dim.314), calls=%async_computation | async-start | bytes 1048576 | tf_op jit(solution)/shard_map/all_to_all | solution.py:16
  28.1 17.6 %all_gather.3 = bf16[32,8,512]{2,1,0:T(8,128)(2,1)S(1)} all-gather(bf16[2,8,512]{2,1,0:T(8,128)(2,1)S(1)} %fusion.38), channel_id=1, replica_groups=mesh['row'=16,'col'=32] {'row'}, dimensions={0}, use_global_device_ids=true | all-gather | bytes 278528 | tf_op jit(solution)/shard_map/all_gather | solution.py:118
  45.7 0.5 slice_convert_fusion.31
  46.3 2.1 %fusion.24 = (f32[256,512]{1,0:T(8,128)S(1)}, f32[256,512]{1,0:T(8,128)S(1)}) fusion(s32[512]{0:T(512)S(1)} %iota_add_fusion, s32[256]{0:T(256)S(1)} %iota_add_fusion.1), kind=kLoop, calls=%fused_computation.36 | loop fusion | flops 1966080 | bytes 1051648 | tf_op jit(solution)/shard_map/cos | solution.py:46
  48.4 12.7 %all-to-all-done = bf16[32,2,8,512]{3,2,1,0:T(8,128)(2,1)S(1)} async-done(((bf16[32,2,8,512]{3,2,1,0:T(8,128)(2,1)}), bf16[32,2,8,512]{3,2,1,0:T(8,128)(2,1)S(1)}, u32[]{:S(2)}, u32[]{:S(2)}) %all-to-all-start) | async-done | bytes 524320 | tf_op jit(solution)/shard_map/all_to_all | solution.py:16
  61.1 1.0 %slice_convert_fusion.15 = (f32[64,1,256]{2,1,0:T(1,128)S(1)}, f32[64,1,256]{2,1,0:T(1,128)S(1)}, f32[64,1,256]{2,1,0:T(1,128)S(1)}, f32[64,1,256]{2,1,0:T(1,128...) fusion(bf16[64,8,512]{2,1,0:T(8,128)(2,1)S(1)} %bitcast.117), kind=kLoop, calls=%fused_computation.52 | loop fusion | flops 262144 | bytes 1572864 | tf_op jit(solution)/shard_map/mul | solution.py:105
  62.2 2.2 %add_add_fusion = f32[64,32,256]{2,1,0:T(8,128)S(1)} fusion(f32[32,256]{1,0:T(8,128)S(1)} %get-tuple-element.70, f32[64,256]{1,0:T(8,128)S(1)} %get-tuple-element.86, f32[32,256]{1,0:T(8,128)S(1)} %get-tuple-element.71, f32[64,256]{1,0:T(8,128)S(1)} %get-tuple-element.87, f32[32,256]{1,0:T(8,128)S(1)} %get-tuple-element.72, ...), kind=kLoop, calls=%fused_computation.9 | loop fusion | flops 16252928 | bytes 3670016 | tf_op jit(solution)/shard_map/add | solution.py:106
  64.4 2.2 %add_add_fusion.1 = f32[64,32,256]{2,1,0:T(8,128)S(1)} fusion(f32[32,256]{1,0:T(8,128)S(1)} %get-tuple-element.70, f32[64,256]{1,0:T(8,128)S(1)} %get-tuple-element.86, f32[32,256]{1,0:T(8,128)S(1)} %get-tuple-element.71, f32[64,256]{1,0:T(8,128)S(1)} %get-tuple-element.87, f32[32,256]{1,0:T(8,128)S(1)} %get-tuple-element.72, ...), kind=kLoop, calls=%fused_computation.10 | loop fusion | flops 16252928 | bytes 3670016 | tf_op jit(solution)/shard_map/add | solution.py:105
  66.7 7.0 %fusion.4 = bf16[2048,512]{1,0:T(8,128)(2,1)S(1)} fusion(f32[2048,256]{1,0:T(8,128)S(1)} %bitcast.118, f32[2048,256]{1,0:T(8,128)S(1)} %bitcast.119, f32[256,512]{1,0:T(8,128)S(1)} %get-tuple-element.55, f32[256,512]{1,0:T(8,128)S(1)} %get-tuple-element.54), kind=kOutput, calls=%fused_computation.4 | convolution fusion | flops 6445072384 | bytes 7340032 | tf_op jit(solution)/shard_map/dot_general | solution.py:108
  73.6 2.2 %reshape_reshape.3 = bf16[64,1,16,2,512]{4,3,2,0,1:T(2,128)(2,1)} reshape(bf16[2048,512]{1,0:T(8,128)(2,1)S(1)} %fusion.4) | data formatting | bytes 4194304 | tf_op jit(solution)/shard_map/reshape;reshape | solution.py:120
  (36 shorter events, 0.3 us)
Async XLA Ops:
  7.4 1.7 %copy-start = (s32[2]{0:T(128)S(1)}, s32[2]{0:T(128)}, u32[]{:S(2)}) copy-start(s32[2]{0:T(128)} %param.8) | copy-start | bytes 28
  7.4 1.7 %copy-start.1 = (s32[2]{0:T(128)S(1)}, s32[2]{0:T(128)}, u32[]{:S(2)}) copy-start(s32[2]{0:T(128)} %param.7) | copy-start | bytes 28
  10.2 51.0 %all-to-all-start = ((bf16[32,2,8,512]{3,2,1,0:T(8,128)(2,1)}), bf16[32,2,8,512]{3,2,1,0:T(8,128)(2,1)S(1)}, u32[]{:S(2)}, u32[]{:S(2)}) async-start(bf16[32,2,8,512]{3,2,1,0:T(8,128)(2,1)} %broadcast_in_dim.314), calls=%async_computation | async-start | bytes 1048576 | tf_op jit(solution)/shard_map/all_to_all | solution.py:16
where the time goes:
time: 76.1 us; the launch traced here: 75.8 us
  starting transfers between devices  17.9 us (24%)
  blocking collectives  17.6 us (23%)
  other arithmetic  13.8 us (18%)
  waiting for transfers between devices  12.7 us (17%)
  matrix products  8.27 us (11%)
  local copies, waits for them, and re-layouts  5.18 us (7%)
    all_to_all x1, starting transfers between devices, sent_to_all(): lax.all_to_all(jnp.broadcast_to(x[None], (devices, *x.shape)), axis, 0, 0...  17.9 us
    all_gather x1, blocking collectives, body(): lax.all_gather(white, 'row', axis=0, tiled=True)  17.6 us
    all_to_all x1, waiting for transfers between devices, sent_to_all(): lax.all_to_all(jnp.broadcast_to(x[None], (devices, *x.shape)), axis, 0, 0...  12.7 us
    dot_general x1, matrix products, correlate(): jnp.dot(cross.reshape(count_i * count_j, 2 * BINS), table, precision=lax....  6.96 us
    cos x1, other arithmetic, transform_table(): jnp.cos(phase)  4.13 us
    another operation x1, local copies, waits for them, and re-layouts, body(): stacked.reshape(stacked.shape[0], 1, lax.axis_size('row'), channel_count,...  2.21 us
    add x1, other arithmetic, correlate(): cross_im = cross_im + (left_im * right_re - left_re * right_im)  2.21 us
    add x1, other arithmetic, correlate(): cross_re = cross_re + (left_re * right_re + left_im * right_im)  2.21 us
  transfers between devices with their start and end apart: 1, of which 1 were waited for; matrix products, arithmetic and copies ran while one was open for 4% of the time, Pallas kernels for 0%

commit v1 on v0

--- a/solution.py
+++ b/solution.py
@@ -115,7 +115,13 @@
     white = whiten(traces, offsets, band_lo, band_hi, live)
     table = lag_table()
     first_panel = gather_directly(white, "col", 0)
-    stacked = correlate(first_panel, lax.all_gather(white, "row", axis=0, tiled=True), table)
+    stacked = correlate(
+        first_panel,
+        jnp.concatenate(
+            lax.all_to_all(jnp.stack([white] * lax.axis_size("row")), "row", 0, 0), axis=0
+        ),
+        table,
+    )
     channel_count = white.shape[0]
     return stacked.reshape(stacked.shape[0], 1, lax.axis_size("row"), channel_count, LAGS)
 

time: 76.1 us -> 90.1 us (1.18)
  the two profiles are of different devices: /device:TPU:24 before, /device:TPU:4 now
where the time goes in v1:
time: 90.1 us; the launch traced here: 89.7 us
  waiting for transfers between devices  37.7 us (42%)
  starting transfers between devices  23.4 us (26%)
  other arithmetic  13.8 us (15%)
  matrix products  8.27 us (9%)
  local copies, waits for them, and re-layouts  6.13 us (7%)
    all_to_all x1, waiting for transfers between devices, sent_to_all(): lax.all_to_all(jnp.broadcast_to(x[None], (devices, *x.shape)), axis, 0, 0...  31.8 us
    all_to_all x1, starting transfers between devices, sent_to_all(): lax.all_to_all(jnp.broadcast_to(x[None], (devices, *x.shape)), axis, 0, 0...  18.2 us
    dot_general x1, matrix products, correlate(): jnp.dot(cross.reshape(count_i * count_j, 2 * BINS), table, precision=lax....  6.96 us
    all_to_all x1, waiting for transfers between devices, body(): lax.all_to_all(jnp.stack([white] * lax.axis_size('row')), 'row', 0, 0)  5.87 us
    all_to_all x1, starting transfers between devices, body(): lax.all_to_all(jnp.stack([white] * lax.axis_size('row')), 'row', 0, 0)  5.21 us
    cos x1, other arithmetic, transform_table(): jnp.cos(phase)  4.13 us
    another operation x1, local copies, waits for them, and re-layouts, body(): stacked.reshape(stacked.shape[0], 1, lax.axis_size('row'), channel_count,...  2.21 us
    add x1, other arithmetic, correlate(): cross_im = cross_im + (left_im * right_re - left_re * right_im)  2.21 us
  transfers between devices with their start and end apart: 2, of which 2 were waited for; matrix products, arithmetic and copies ran while one was open for 3% of the time, Pallas kernels for 0%

profile of v1, /device:TPU:4, one launch (start us, length us, event | category | flops | bytes accessed | tf_op | source)
XLA Modules:
  0.0 89.7 jit_solution(15936133761434163184)
XLA Ops:
  0.0 0.7 broadcast_compare_fusion.13
  0.7 0.7 broadcast_compare_fusion.9
  1.4 0.1 broadcast_in_dim.248
  1.5 0.1 broadcast_in_dim.253
  1.6 0.1 broadcast_in_dim.303
  1.7 0.1 broadcast_in_dim.298
  1.8 0.1 broadcast_in_dim.293
  1.8 0.1 broadcast_in_dim.288
  1.9 0.1 broadcast_in_dim.283
  2.0 0.1 broadcast_in_dim.278
  2.1 0.1 broadcast_in_dim.273
  2.2 0.1 broadcast_in_dim.268
  2.3 0.1 broadcast_in_dim.263
  2.4 0.1 broadcast_in_dim.258
  2.4 0.1 broadcast_in_dim.308
  2.5 0.8 copy.79
  3.3 4.1 %fusion.23 = (f32[1024,256]{1,0:T(8,128)S(1)}, f32[1024,256]{1,0:T(8,128)S(1)}) fusion(s32[256]{0:T(256)S(1)} %iota_add_fusion.1), kind=kLoop, calls=%fused_computation.35 | loop fusion | flops 3932160 | bytes 2098176 | tf_op jit(solution)/shard_map/cos | solution.py:37
  7.4 0.0 copy-start
  7.4 0.0 copy-start.1
  7.6 1.3 %fusion.7 = f32[16,512]{1,0:T(8,128)S(1)} fusion(f32[1024,256]{1,0:T(8,128)S(1)} %get-tuple-element.69, f32[1024,256]{1,0:T(8,128)S(1)} %get-tuple-element.68, f32[1024]{0:T(1024)S(1)} %multiply_subtract_fusion, f32[16,1024]{1,0:T(8,128)S(1)} %bitcast.135, f32[16,1024]{1,0:T(8,128)S(1)} %bitcast.134, f32[16,1024]{1,0:T(8,128)S(1)} %bitcast.133, ...), kind=kOutput, calls=%fused_computation.6 | convolution fusion | flops 101924864 | bytes 2986192 | tf_op jit(solution)/shard_map/dot_general | solution.py:67
  9.0 0.1 fusion.67
  9.1 0.0 copy-done
  9.1 0.0 copy-done.1
  9.1 0.1 and_convert_fusion
  9.2 0.1 bitcast_multiply_fusion
  9.3 0.9 %stack.2 = bf16[16,2,8,512]{3,1,2,0:T(2,128)(2,1)} broadcast(bf16[2,8,512]{2,0,1:T(2,128)(2,1)S(1)} %copy.10), dimensions={1,2,3} | broadcast | bytes 278528 | tf_op jit(solution)/shard_map/stack | solution.py:121
  10.2 5.2 %all-to-all-start.1 = ((bf16[16,2,8,512]{3,1,2,0:T(2,128)(2,1)}), bf16[16,2,8,512]{3,1,2,0:T(2,128)(2,1)S(1)}, u32[]{:S(2)}, u32[]{:S(2)}) async-start(bf16[16,2,8,512]{3,1,2,0:T(2,128)(2,1)} %stack.2), calls=%async_computation.1 | async-start | bytes 524288 | tf_op jit(solution)/shard_map/all_to_all | solution.py:121
  15.5 2.1 %fusion.24 = (f32[256,512]{1,0:T(8,128)S(1)}, f32[256,512]{1,0:T(8,128)S(1)}) fusion(s32[512]{0:T(512)S(1)} %iota_add_fusion, s32[256]{0:T(256)S(1)} %iota_add_fusion.1), kind=kLoop, calls=%fused_computation.36 | loop fusion | flops 1966080 | bytes 1051648 | tf_op jit(solution)/shard_map/cos | solution.py:46
  17.6 5.9 %all-to-all-done.1 = bf16[16,2,8,512]{3,1,2,0:T(2,128)(2,1)S(1)} async-done(((bf16[16,2,8,512]{3,1,2,0:T(2,128)(2,1)}), bf16[16,2,8,512]{3,1,2,0:T(2,128)(2,1)S(1)}, u32[]{:S(2)}, u32[]{:S(2)}) %all-to-all-start.1) | async-done | bytes 262176 | tf_op jit(solution)/shard_map/all_to_all | solution.py:121
  23.5 0.9 broadcast_in_dim.314
  24.3 18.2 %all-to-all-start = ((bf16[32,2,8,512]{3,2,1,0:T(8,128)(2,1)}), bf16[32,2,8,512]{3,2,1,0:T(8,128)(2,1)S(1)}, u32[]{:S(2)}, u32[]{:S(2)}) async-start(bf16[32,2,8,512]{3,2,1,0:T(8,128)(2,1)} %broadcast_in_dim.314), calls=%async_computation | async-start | bytes 1048576 | tf_op jit(solution)/shard_map/all_to_all | solution.py:16
  42.6 0.5 slice_convert_fusion.31
  43.2 31.8 %all-to-all-done = bf16[32,2,8,512]{3,2,1,0:T(8,128)(2,1)S(1)} async-done(((bf16[32,2,8,512]{3,2,1,0:T(8,128)(2,1)}), bf16[32,2,8,512]{3,2,1,0:T(8,128)(2,1)S(1)}, u32[]{:S(2)}, u32[]{:S(2)}) %all-to-all-start) | async-done | bytes 524320 | tf_op jit(solution)/shard_map/all_to_all | solution.py:16
  75.0 1.0 %slice_convert_fusion.15 = (f32[64,1,256]{2,1,0:T(1,128)S(1)}, f32[64,1,256]{2,1,0:T(1,128)S(1)}, f32[64,1,256]{2,1,0:T(1,128)S(1)}, f32[64,1,256]{2,1,0:T(1,128...) fusion(bf16[64,8,512]{2,1,0:T(8,128)(2,1)S(1)} %bitcast.118), kind=kLoop, calls=%fused_computation.52 | loop fusion | flops 262144 | bytes 1572864 | tf_op jit(solution)/shard_map/mul | solution.py:105
  76.1 2.2 %add_add_fusion = f32[64,32,256]{2,1,0:T(8,128)S(1)} fusion(f32[32,256]{1,0:T(8,128)S(1)} %get-tuple-element.70, f32[64,256]{1,0:T(8,128)S(1)} %get-tuple-element.86, f32[32,256]{1,0:T(8,128)S(1)} %get-tuple-element.71, f32[64,256]{1,0:T(8,128)S(1)} %get-tuple-element.87, f32[32,256]{1,0:T(8,128)S(1)} %get-tuple-element.72, ...), kind=kLoop, calls=%fused_computation.9 | loop fusion | flops 16252928 | bytes 3670016 | tf_op jit(solution)/shard_map/add | solution.py:106
  78.3 2.2 %add_add_fusion.1 = f32[64,32,256]{2,1,0:T(8,128)S(1)} fusion(f32[32,256]{1,0:T(8,128)S(1)} %get-tuple-element.70, f32[64,256]{1,0:T(8,128)S(1)} %get-tuple-element.86, f32[32,256]{1,0:T(8,128)S(1)} %get-tuple-element.71, f32[64,256]{1,0:T(8,128)S(1)} %get-tuple-element.87, f32[32,256]{1,0:T(8,128)S(1)} %get-tuple-element.72, ...), kind=kLoop, calls=%fused_computation.10 | loop fusion | flops 16252928 | bytes 3670016 | tf_op jit(solution)/shard_map/add | solution.py:105
  80.5 7.0 %fusion.4 = bf16[2048,512]{1,0:T(8,128)(2,1)S(1)} fusion(f32[2048,256]{1,0:T(8,128)S(1)} %bitcast.120, f32[2048,256]{1,0:T(8,128)S(1)} %bitcast.121, f32[256,512]{1,0:T(8,128)S(1)} %get-tuple-element.55, f32[256,512]{1,0:T(8,128)S(1)} %get-tuple-element.54), kind=kOutput, calls=%fused_computation.4 | convolution fusion | flops 6445072384 | bytes 7340032 | tf_op jit(solution)/shard_map/dot_general | solution.py:108
  87.5 2.2 %reshape_reshape.3 = bf16[64,1,16,2,512]{4,3,2,0,1:T(2,128)(2,1)} reshape(bf16[2048,512]{1,0:T(8,128)(2,1)S(1)} %fusion.4) | data formatting | bytes 4194304 | tf_op jit(solution)/shard_map/reshape;reshape | solution.py:126
  (38 shorter events, 0.4 us)
Async XLA Ops:
  7.4 1.7 %copy-start = (s32[2]{0:T(128)S(1)}, s32[2]{0:T(128)}, u32[]{:S(2)}) copy-start(s32[2]{0:T(128)} %param.8) | copy-start | bytes 28
  7.4 1.7 %copy-start.1 = (s32[2]{0:T(128)S(1)}, s32[2]{0:T(128)}, u32[]{:S(2)}) copy-start(s32[2]{0:T(128)} %param.7) | copy-start | bytes 28
  10.2 13.2 %all-to-all-start.1 = ((bf16[16,2,8,512]{3,1,2,0:T(2,128)(2,1)}), bf16[16,2,8,512]{3,1,2,0:T(2,128)(2,1)S(1)}, u32[]{:S(2)}, u32[]{:S(2)}) async-start(bf16[16,2,8,512]{3,1,2,0:T(2,128)(2,1)} %stack.2), calls=%async_computation.1 | async-start | bytes 524288 | tf_op jit(solution)/shard_map/all_to_all | solution.py:121
  24.3 50.7 %all-to-all-start = ((bf16[32,2,8,512]{3,2,1,0:T(8,128)(2,1)}), bf16[32,2,8,512]{3,2,1,0:T(8,128)(2,1)S(1)}, u32[]{:S(2)}, u32[]{:S(2)}) async-start(bf16[32,2,8,512]{3,2,1,0:T(8,128)(2,1)} %broadcast_in_dim.314), calls=%async_computation | async-start | bytes 1048576 | tf_op jit(solution)/shard_map/all_to_all | solution.py:16
